TPU v7x, 32 devices: a whole 2x2x4 slice. The times are simulated.
32 devices in a mesh: groups: 2 (over y), ep: 8 (over z, x), tp: 2 (over core).
Axes of the slice: x: 2, y: 2, z: 4, core: 2. Of those that a mesh axis runs over, the one named last changes fastest.
Arguments:
- hidden: bfloat16 [128, 4096], P(('groups', 'ep', 'tp')), parts along dimension 0, may hold values from -6 to 6
- norm_gain: float32 [4096], replicated, may hold values from 0.5 to 1.5
- rot_left: float32 [64, 64], replicated, may hold values from -0.75 to 0.75
- rot_right: float32 [64, 64], replicated, may hold values from -0.75 to 0.75
- expert_ids: int32 [128, 8], P(('groups', 'ep')), parts along dimension 0, may hold values from 0 to 63, as said below
- gate_weights: float32 [128, 8], P(('groups', 'ep')), parts along dimension 0, may hold values from 0.05 to 1
- w_gate: bfloat16 [128, 4096, 384], P('ep', 'tp'), may hold values from -0.09375 to 0.09375
- w_up: bfloat16 [128, 4096, 384], P('ep', 'tp'), may hold values from -0.09375 to 0.09375
- w_down: bfloat16 [128, 384, 4096], P('ep', None, 'tp'), may hold values from -0.21875 to 0.21875
- unit_scales: float32 [128, 2, 384], P('ep'), may hold values from 0.25 to 1.75
Outputs:
- moe_out: bfloat16 [128, 4096], P(('groups', 'ep', 'tp')), parts along dimension 0
There are 2 independent parts, one for each index of `groups`. A program takes and returns all parts, laid end to end along the dimension named above; an argument that names none is the same for every part. Nothing has to cross between parts.
Inputs may be any that keep to these rules, and one draw needn't show every extreme that they name: `expert_ids`: each row names 8 different experts. In each aligned block of 8 rows (the rows of one index of ep) no expert is named by more than 2 rows, and in every block some experts are named by exactly 2 rows; every expert is named by exactly 2 rows in some block.
All inputs are finite; a program needn't handle non-finite values.
Results may differ from a plain program's by a relative error of at most 0.0082.
Values may be sent and summed in bfloat16 or wider, within the bound.
A program may use at most 128 MiB of HBM per device.

v0:
```python
import jax
import jax.numpy as jnp
from jax import lax
from jax.sharding import PartitionSpec as P

EXPERTS = 64


def rotate(hidden, norm_gain, rot_left, rot_right):
    values = hidden.astype(jnp.float32)
    mean_square = jnp.mean(values * values, axis=1, keepdims=True)
    normed = values * lax.rsqrt(mean_square + 1e-06) * norm_gain[None, :]
    factor = rot_left.shape[0]
    square = normed.reshape(-1, factor, factor)
    turned = jnp.einsum("ij,rjk->rik", rot_left, square, precision=lax.Precision.HIGHEST)
    turned = jnp.einsum("rik,lk->ril", turned, rot_right, precision=lax.Precision.HIGHEST)
    return turned.reshape(normed.shape).astype(jnp.bfloat16)


def activate(gate_sum, up_sum, unit_scales):
    gate_scale = unit_scales[None, :, 0, None, :]
    up_scale = unit_scales[None, :, 1, None, :]
    return (jax.nn.silu(gate_sum * gate_scale) * (up_sum * up_scale)).astype(jnp.bfloat16)


def body(
    hidden,
    norm_gain,
    rot_left,
    rot_right,
    expert_ids,
    gate_weights,
    w_gate,
    w_up,
    w_down,
    unit_scales,
):
    ep_count = lax.axis_size("ep")
    group_rows = expert_ids.shape[0]
    top_count = expert_ids.shape[1]
    held_halves = w_gate.shape[0]
    capacity = 5 * group_rows * top_count // (2 * EXPERTS)
    rotated = rotate(hidden, norm_gain, rot_left, rot_right)
    pair_rows = lax.all_to_all(rotated, "tp", split_axis=1, concat_axis=0, tiled=True)
    weight_norm = (gate_weights / jnp.sum(gate_weights, axis=1, keepdims=True)).astype(jnp.bfloat16)
    onehot = (
        expert_ids.reshape(-1)[:, None] == jnp.arange(EXPERTS, dtype=jnp.int32)[None, :]
    ).astype(jnp.int32)
    slot_rank = jnp.sum((jnp.cumsum(onehot, axis=0) - onehot) * onehot, axis=1).reshape(
        group_rows, top_count
    )
    low_target = expert_ids * capacity + slot_rank
    targets = (low_target, low_target + EXPERTS * capacity)
    line_count = 2 * EXPERTS * capacity
    line_index = jnp.arange(line_count, dtype=jnp.int32)[:, None, None]
    matches = jnp.zeros((line_count, group_rows, top_count), jnp.float32)
    for target in targets:
        matches = matches + (line_index == target[None, :, :]).astype(jnp.float32)
    dispatch = jnp.sum(matches, axis=2).astype(jnp.bfloat16)
    outgoing = jnp.dot(dispatch, pair_rows, preferred_element_type=jnp.float32).astype(jnp.bfloat16)
    outgoing = outgoing.reshape(ep_count, held_halves * capacity, -1)
    received = lax.all_to_all(outgoing, "ep", split_axis=0, concat_axis=0, tiled=True)
    received = received.reshape(ep_count, held_halves, capacity, -1)
    gate_sum = jnp.einsum("shcd,hdf->shcf", received, w_gate, preferred_element_type=jnp.float32)
    up_sum = jnp.einsum("shcd,hdf->shcf", received, w_up, preferred_element_type=jnp.float32)
    gate_sum, up_sum = (
        lax.psum_scatter(gate_sum, "tp", scatter_dimension=0, tiled=True),
        lax.psum_scatter(up_sum, "tp", scatter_dimension=0, tiled=True),
    )
    half_hidden = activate(gate_sum, up_sum, unit_scales)
    hidden_units = lax.all_gather(half_hidden, "tp", axis=0, tiled=True)
    partial_value = jnp.einsum(
        "shcf,hfd->shcd", hidden_units, w_down, preferred_element_type=jnp.float32
    ).astype(jnp.bfloat16)
    flat_partial = partial_value.reshape(ep_count, held_halves * capacity, -1)
    returned = lax.all_to_all(flat_partial, "ep", split_axis=0, concat_axis=0, tiled=True)
    returned = returned.reshape(2 * EXPERTS * capacity, -1)
    expert_out = (
        returned[: EXPERTS * capacity].astype(jnp.float32)
        + returned[EXPERTS * capacity :].astype(jnp.float32)
    ).astype(jnp.bfloat16)
    line_spot = (expert_ids * capacity + slot_rank)[:, :, None]
    out_lines = EXPERTS * capacity
    columns = jnp.arange(out_lines, dtype=jnp.int32)[None, None, :]
    hits = (columns == line_spot).astype(jnp.float32)
    mixing = jnp.sum(weight_norm.astype(jnp.float32)[:, :, None] * hits, axis=1).astype(
        jnp.bfloat16
    )
    combined = jnp.dot(mixing, expert_out, preferred_element_type=jnp.float32).astype(jnp.bfloat16)
    return lax.all_to_all(combined, "tp", split_axis=0, concat_axis=1, tiled=True)


def solution(mesh):
    placed = (
        P(("groups", "ep", "tp"), None),
        P(),
        P(),
        P(),
        P(("groups", "ep"), None),
        P(("groups", "ep"), None),
        P("ep", "tp", None),
        P("ep", "tp", None),
        P("ep", None, "tp"),
        P("ep", None, None),
    )
    return jax.shard_map(
        body, mesh=mesh, in_specs=placed, out_specs=P(("groups", "ep", "tp"), None), check_vma=False
    )
```

profile of v0, /device:TPU:0, one launch (start us, length us, event | category | flops | bytes accessed | tf_op | source)
XLA Modules:
  0.0 139.3 jit_solution(9439551862724553802)
XLA Ops:
  6.5 0.9 fusion.16
  7.5 0.8 fusion.17
  8.4 0.4 convolution_bitcast_fusion
  8.8 1.1 convolution_convert_fusion.2
  10.1 0.6 copy.32
  10.7 3.3 %all-to-all-start = ((bf16[4,2,2048]{2,0,1:T(4,128)(2,1)}), bf16[4,2,2048]{2,0,1:T(4,128)(2,1)S(1)}, u32[]{:S(2)}, u32[]{:S(2)}) async-start(bf16[4,2,2048]{2,0,1:T(4,128)(2,1)} %copy.32), calls=%async_computation | async-start | bytes 65536 | tf_op jit(solution)/shard_map/all_to_all | solution.py:44
  14.1 0.8 eq.27
  15.3 0.7 broadcast_add_fusion
  16.1 0.5 convolution_convert_fusion
  16.6 33.4 %all_to_all.45 = bf16[8,32,2048]{2,1,0:T(8,128)(2,1)S(1)} all-to-all(bf16[8,32,2048]{2,1,0:T(8,128)(2,1)S(1)} %bitcast.58), channel_id=1, replica_groups=mesh['groups'=2,'ep'=8,'tp'=2] {'ep'}, dimensions={0} | all-to-all | bytes 2097152 | tf_op jit(solution)/shard_map/all_to_all | solution.py:62
  50.0 0.6 copy.33
  50.6 9.9 %fusion.9 = f32[8,16,2,384]{3,0,2,1:T(8,128)S(1)} fusion(bf16[8,16,2,2048]{3,0,2,1:T(8,128)(2,1)S(1)} %bitcast.55, bf16[16,2048,384]{2,1,0:T(8,128)(2,1)} %param.16), kind=kOutput, calls=%fused_computation.9 | convolution fusion | flops 402653184 | bytes 26607616 | tf_op jit(solution)/shard_map/shcd,hdf->shcf/dot_general | solution.py:64
  60.5 0.9 copy.34
  61.4 10.1 %fusion.12 = f32[8,16,2,384]{3,0,2,1:T(8,128)S(1)} fusion(bf16[8,16,2,2048]{3,0,2,1:T(8,128)(2,1)S(1)} %bitcast.56, bf16[16,2048,384]{2,1,0:T(8,128)(2,1)} %param.17), kind=kOutput, calls=%fused_computation.10 | convolution fusion | flops 402653184 | bytes 26607616 | tf_op jit(solution)/shard_map/shcd,hdf->shcf/dot_general | solution.py:65
  71.6 0.9 copy.36
  72.6 7.1 %reduce-scatter.5.cloned.1.call-done = f32[4,16,2,384]{3,1,2,0:T(8,128)} async-done(((f32[8,16,2,384]{3,1,2,0:T(8,128)}), f32[4,16,2,384]{3,1,2,0:T(8,128)}) %reduce-scatter.5.cloned.1.call-update) | async-done | bytes 196624 | tf_op jit(solution)/shard_map/reduce_scatter | solution.py:68
  79.6 1.1 multiply_convert_fusion
  80.7 1.9 %all_gather.3 = bf16[8,16,2,384]{3,1,2,0:T(8,128)(2,1)S(1)} all-gather(bf16[4,16,2,384]{3,1,2,0:T(8,128)(2,1)S(1)} %multiply_convert_fusion), channel_id=1, replica_groups=mesh['groups'=2,'ep'=8,'tp'=2] {'tp'}, dimensions={0}, use_global_device_ids=true | all-gather | bytes 294912 | tf_op jit(solution)/shard_map/all_gather | solution.py:71
  82.7 11.5 %fusion.6 = bf16[16,8,2,2048]{3,1,2,0:T(8,128)(2,1)S(1)} fusion(bf16[16,384,2048]{2,1,0:T(8,128)(2,1)} %param.18, bf16[8,16,2,384]{3,1,2,0:T(8,128)(2,1)S(1)} %all_gather.3), kind=kOutput, calls=%fused_computation.6 | convolution fusion | flops 403177472 | bytes 26411008 | tf_op jit(solution)/shard_map/shcf,hfd->shcd/dot_general | solution.py:72
  94.2 1.6 %copy.39 = bf16[8,32,2048]{2,1,0:T(8,128)(2,1)} copy(bf16[8,32,2048]{2,0,1:T(8,128)(2,1)S(1)} %bitcast.57) | data formatting | bytes 2097152 | tf_op jit(solution)/shard_map/reshape | solution.py:75
  95.8 5.7 %all-to-all-start.2 = ((bf16[8,32,2048]{2,1,0:T(8,128)(2,1)}), bf16[8,32,2048]{2,1,0:T(8,128)(2,1)S(1)}, u32[]{:S(2)}, u32[]{:S(2)}) async-start(bf16[8,32,2048]{2,1,0:T(8,128)(2,1)} %copy.39), calls=%async_computation.4 | async-start | bytes 2097152 | tf_op jit(solution)/shard_map/all_to_all | solution.py:76
  101.8 26.0 %all-to-all-done.2 = bf16[8,32,2048]{2,1,0:T(8,128)(2,1)S(1)} async-done(((bf16[8,32,2048]{2,1,0:T(8,128)(2,1)}), bf16[8,32,2048]{2,1,0:T(8,128)(2,1)S(1)}, u32[]{:S(2)}, u32[]{:S(2)}) %all-to-all-start.2) | async-done | bytes 1048608 | tf_op jit(solution)/shard_map/all_to_all | solution.py:76
  128.1 3.7 %all_to_all.46 = bf16[2,4,2048]{2,1,0:T(4,128)(2,1)S(1)} all-to-all(bf16[2,4,2048]{2,1,0:T(4,128)(2,1)S(1)} %all_to_all.37), channel_id=1, replica_groups=mesh['groups'=2,'ep'=8,'tp'=2] {'tp'}, dimensions={0} | all-to-all | bytes 65536 | tf_op jit(solution)/shard_map/all_to_all | solution.py:90
  131.9 0.6 copy.53
  (31 shorter events, 1.6 us)
Async XLA Ops:
  6.5 1.9 %copy-start = (f32[64,64]{1,0:T(8,128)S(1)}, f32[64,64]{1,0:T(8,128)}, u32[]{:S(2)}) copy-start(f32[64,64]{1,0:T(8,128)} %param.12) | copy-start | bytes 49156
  10.7 5.2 %all-to-all-start = ((bf16[4,2,2048]{2,0,1:T(4,128)(2,1)}), bf16[4,2,2048]{2,0,1:T(4,128)(2,1)S(1)}, u32[]{:S(2)}, u32[]{:S(2)}) async-start(bf16[4,2,2048]{2,0,1:T(4,128)(2,1)} %copy.32), calls=%async_computation | async-start | bytes 65536 | tf_op jit(solution)/shard_map/all_to_all | solution.py:44
  14.0 58.5 %reduce-scatter.3.cloned.1.call-start = ((), (), s32[]{:S(2)}) async-start(), calls=%async_computation.6 | async-start | bytes 589824 | tf_op jit(solution)/shard_map/reduce_scatter | solution.py:67
  50.6 21.9 %copy-start.2 = (f32[16,2,384]{2,1,0:T(2,128)S(1)}, f32[16,2,384]{2,1,0:T(2,128)}, u32[]{:S(2)}) copy-start(f32[16,2,384]{2,1,0:T(2,128)} %param.19) | copy-start | bytes 147460
  61.4 18.3 %reduce-scatter.5.cloned.1.call-start = ((), (), s32[]{:S(2)}) async-start(), calls=%async_computation.7 | async-start | bytes 589824 | tf_op jit(solution)/shard_map/reduce_scatter | solution.py:68
  61.4 71.1 %copy-start.1 = (f32[64,64]{1,0:T(8,128)S(1)}, f32[64,64]{1,0:T(8,128)}, u32[]{:S(2)}) copy-start(f32[64,64]{1,0:T(8,128)} %param.12) | copy-start | bytes 49156
  71.6 30.0 %copy-start.3 = (f32[8,8]{1,0:T(8,128)S(1)}, f32[8,8]{1,0:T(8,128)}, u32[]{:S(2)}) copy-start(f32[8,8]{1,0:T(8,128)} %param.15) | copy-start | bytes 772
  95.8 32.0 %all-to-all-start.2 = ((bf16[8,32,2048]{2,1,0:T(8,128)(2,1)}), bf16[8,32,2048]{2,1,0:T(8,128)(2,1)S(1)}, u32[]{:S(2)}, u32[]{:S(2)}) async-start(bf16[8,32,2048]{2,1,0:T(8,128)(2,1)} %copy.39), calls=%async_computation.4 | async-start | bytes 2097152 | tf_op jit(solution)/shard_map/all_to_all | solution.py:76
Sparse Core Ops, SparseCore 0:
  61.5 6.8 reduce-scatter.2
  72.6 7.0 reduce-scatter.4
where the time goes:
time: 140 us; the launch traced here: 139 us
  blocking collectives  39.1 us (28%)
  matrix products  33.7 us (24%)
  waiting for transfers between devices  33.1 us (24%)
  between operations  13.6 us (10%)
  starting transfers between devices  9.08 us (6%)
  local copies, waits for them, and re-layouts  6.33 us (5%)
  other arithmetic  4.44 us (3%)
    all_to_all x1, blocking collectives, body(): lax.all_to_all(outgoing, 'ep', split_axis=0, concat_axis=0, tiled=True)  33.4 us
    all_to_all x1, waiting for transfers between devices, body(): lax.all_to_all(flat_partial, 'ep', split_axis=0, concat_axis=0, tiled=True)  26 us
    dot_general x1, matrix products, body(): jnp.einsum('shcf,hfd->shcd', hidden_units, w_down, preferred_element_type...  11.5 us
    dot_general x1, matrix products, body(): jnp.einsum('shcd,hdf->shcf', received, w_up, preferred_element_type=jnp.f...  10.1 us
    dot_general x1, matrix products, body(): jnp.einsum('shcd,hdf->shcf', received, w_gate, preferred_element_type=jnp...  9.91 us
    reduce_scatter x1, waiting for transfers between devices, body(): lax.psum_scatter(up_sum, 'tp', scatter_dimension=0, tiled=True)  7.08 us
    all_to_all x1, starting transfers between devices, body(): lax.all_to_all(flat_partial, 'ep', split_axis=0, concat_axis=0, tiled=True)  5.74 us
    all_to_all x1, blocking collectives, body(): lax.all_to_all(combined, 'tp', split_axis=0, concat_axis=1, tiled=True)  3.75 us
  transfers between devices with their start and end apart: 4, of which 2 were waited for; matrix products, arithmetic and copies ran while one was open for 9% of the time, Pallas kernels for 0%

commit v1 on v0

v1 whole, which is shorter than its diff:
```python
import functools

import jax
import jax.numpy as jnp
from jax import lax
from jax.experimental import pallas as pl
from jax.experimental.pallas import tpu as pltpu
from jax.sharding import PartitionSpec as P

MESH = pl.DeviceIdType.MESH
HIGH = lax.Precision.HIGHEST
LANES = 128
LAG = 3
UNIT_RING = 10
DOWN_RING = 8


def iota(shape, dim):
    return lax.broadcasted_iota(jnp.int32, shape, dim)


def rotate(hid_ref, gain_ref, left_ref, right_ref, n_tp):
    values = hid_ref[...].astype(jnp.float32)
    rows, width = values.shape
    half = width // n_tp
    order = left_ref.shape[0]
    mean_square = jnp.mean(values * values, axis=1, keepdims=True)
    normed = values * lax.rsqrt(mean_square + 1e-06) * gain_ref[...]
    stacked = jnp.concatenate([normed[:, h * half : (h + 1) * half] for h in range(n_tp)], axis=0)
    groups = half // LANES
    tall = jnp.concatenate(
        [stacked[:, m * LANES : (m + 1) * LANES] for m in range(groups)], axis=0
    )
    per_lane = LANES // order
    tall = jnp.concatenate(
        [tall[:, p * order : (p + 1) * order] for p in range(per_lane)], axis=0
    )
    count = tall.shape[0]
    block = n_tp * rows

    def line_of(index):
        return (
            (index % block) // rows * (half // order)
            + index // block % groups * per_lane
            + index // (block * groups)
        )

    spread = (line_of(iota((count, order), 0)) == iota((count, order), 1)).astype(jnp.float32)
    dims = (((1,), (1,)), ((), ()))
    wide = lax.dot_general(
        jnp.dot(spread, left_ref[...], precision=HIGH, preferred_element_type=jnp.float32),
        spread,
        dims,
        precision=HIGH,
        preferred_element_type=jnp.float32,
    )
    same_row = iota((count, count), 0) % rows == iota((count, count), 1) % rows
    wide = jnp.where(same_row, wide, 0.0)
    turned = lax.dot_general(
        tall, right_ref[...], dims, precision=HIGH, preferred_element_type=jnp.float32
    )
    turned = jnp.dot(wide, turned, precision=HIGH, preferred_element_type=jnp.float32)
    step = count // per_lane
    flat = jnp.concatenate([turned[p * step : (p + 1) * step] for p in range(per_lane)], axis=1)
    return jnp.concatenate([flat[m * block : (m + 1) * block] for m in range(groups)], axis=1)


def routing(ids_ref, weights_ref, experts, capacity):
    ids = ids_ref[...]
    weights = weights_ref[...]
    rows, choices = ids.shape
    weights = weights / jnp.sum(weights, axis=1, keepdims=True)
    weights = weights.astype(jnp.bfloat16).astype(jnp.float32)
    lane = iota((rows, capacity * experts), 1)
    expert = lane % experts
    named = jnp.zeros(lane.shape, jnp.float32)
    value = jnp.zeros(lane.shape, jnp.float32)
    for k in range(choices):
        hit = (ids[:, k : k + 1] == expert).astype(jnp.float32)
        named = named + hit
        value = value + hit * weights[:, k : k + 1]
    row = iota(lane.shape, 0)
    rank = jnp.zeros(lane.shape, jnp.float32)
    for r in range(rows):
        rank = rank + jnp.where(row > r, named[r : r + 1, :], 0.0)
    return jnp.where(rank == (lane // experts).astype(jnp.float32), value, 0.0)


def kernel(
    sizes,
    hid_ref,
    gain_ref,
    left_ref,
    right_ref,
    ids_ref,
    weights_ref,
    scales_ref,
    gate_hbm,
    up_hbm,
    down_hbm,
    out_ref,
    gate_buf,
    up_buf,
    down_buf,
    row_out,
    row_in,
    route_out,
    route_in,
    rows_f32,
    route_t,
    lines,
    part_out,
    part_in,
    values,
    back_out,
    back_in,
    gate_sem,
    up_sem,
    down_sem,
    part_send,
    part_recv,
    plain_sem,
):
    n_ep, n_tp, capacity = sizes
    peers = n_ep * n_tp
    ep = lax.axis_index("ep")
    tp = lax.axis_index("tp")
    me = ep * n_tp + tp
    held = gate_hbm.shape[0]
    unit_ring = gate_buf.shape[0]
    down_ring = down_buf.shape[0]
    rows = hid_ref.shape[0]
    half = row_in.shape[2]
    block = rows * n_tp
    slots = capacity * n_ep
    ff = gate_hbm.shape[2]
    experts = held * n_ep // 2
    total_rows = n_ep * block

    def unit_copies(j, slot):
        return (
            pltpu.make_async_copy(gate_hbm.at[j], gate_buf.at[slot], gate_sem.at[slot]),
            pltpu.make_async_copy(up_hbm.at[j], up_buf.at[slot], up_sem.at[slot]),
        )

    def down_copy(j, slot):
        return pltpu.make_async_copy(down_hbm.at[j], down_buf.at[slot], down_sem.at[slot])

    for j in range(max(unit_ring, down_ring + LAG)):
        if j < unit_ring:
            for copy in unit_copies(j, j):
                copy.start()
        if LAG <= j < down_ring + LAG:
            down_copy(j - LAG, j - LAG).start()

    barrier = pltpu.get_barrier_semaphore()

    def peer_of(offset):
        peer = lax.rem(me + offset, peers)
        return {"ep": peer // n_tp, "tp": lax.rem(peer, n_tp)}, peer

    @pl.loop(1, peers)
    def _(offset):
        where, _peer = peer_of(offset)
        pl.semaphore_signal(barrier, inc=1, device_id=where, device_id_type=MESH)

    route = routing(ids_ref, weights_ref, experts, capacity)
    route_out[...] = route
    route_in[ep] = route
    rotated = rotate(hid_ref, gain_ref, left_ref, right_ref, n_tp).astype(jnp.float32)
    for h in range(n_tp):
        row_out[h] = rotated[h * rows : (h + 1) * rows].astype(jnp.bfloat16)
    row_in[me] = row_out[tp]

    pl.semaphore_wait(barrier, peers - 1)

    @pl.loop(1, n_ep)
    def _(offset):
        pltpu.make_async_remote_copy(
            src_ref=route_out,
            dst_ref=route_in.at[ep],
            send_sem=plain_sem.at[0],
            recv_sem=plain_sem.at[1],
            device_id={"ep": lax.rem(ep + offset, n_ep), "tp": tp},
            device_id_type=MESH,
        ).start()

    @pl.loop(1, peers)
    def _(offset):
        where, peer = peer_of(offset)
        pltpu.make_async_remote_copy(
            src_ref=row_out.at[lax.rem(peer, n_tp)],
            dst_ref=row_in.at[me],
            send_sem=plain_sem.at[2],
            recv_sem=plain_sem.at[3],
            device_id=where,
            device_id_type=MESH,
        ).start()

    def drain(ref, count, sem):
        view = ref.at[pl.ds(0, count)]
        pltpu.make_async_copy(view, view, sem).wait()

    drain(route_in, n_ep - 1, plain_sem.at[1])
    route_t[...] = route_in[...].reshape(total_rows, capacity * experts).T
    first = lax.rem(ep * held, experts)
    owner = (iota((n_ep, total_rows), 1) // block == iota((n_ep, total_rows), 0)).astype(jnp.float32)
    picks = []
    for c in range(capacity):
        line = route_t[pl.ds(c * experts + first, held), :]
        picks.append((line[:, None, :] * owner[None, :, :])[:, None])
    weighted = jnp.concatenate(picks, axis=1).reshape(held * slots, total_rows)
    chosen = jnp.where(weighted > 0.0, 1.0, 0.0).astype(jnp.bfloat16)
    mixing = weighted.T.astype(jnp.bfloat16)

    drain(row_in, peers - 1, plain_sem.at[3])

    @pl.loop(0, n_ep)
    def _(b):
        both = [row_in[b * n_tp + h].astype(jnp.float32) for h in range(n_tp)]
        rows_f32[pl.ds(pl.multiple_of(b * block, block), block), :] = jnp.concatenate(both, axis=0)

    lines[...] = (
        jnp.dot(chosen, rows_f32[...].astype(jnp.bfloat16), preferred_element_type=jnp.float32)
        .astype(jnp.bfloat16)
        .reshape(lines.shape)
    )

    def part_copy(j):
        return pltpu.make_async_remote_copy(
            src_ref=part_out.at[j],
            dst_ref=part_in.at[j],
            send_sem=part_send.at[j],
            recv_sem=part_recv.at[j],
            device_id={"ep": ep, "tp": 1 - tp},
            device_id_type=MESH,
        )

    @pl.loop(0, held + LAG)
    def _(t):
        @pl.when(t < held)
        def _():
            slot = lax.rem(t, unit_ring)
            for copy in unit_copies(t, slot):
                copy.wait()
            line = lines[t]
            part_out[t, :, pl.ds(0, ff)] = jnp.dot(
                line, gate_buf[slot], preferred_element_type=jnp.float32
            )
            part_out[t, :, pl.ds(ff, ff)] = jnp.dot(
                line, up_buf[slot], preferred_element_type=jnp.float32
            )
            part_copy(t).start()

            @pl.when(t + unit_ring < held)
            def _():
                for copy in unit_copies(t + unit_ring, slot):
                    copy.start()

        @pl.when(t >= LAG)
        def _():
            j = t - LAG
            slot = lax.rem(j, down_ring)
            part_copy(j).wait_recv()
            scale = scales_ref[j]
            gate = (part_out[j, :, pl.ds(0, ff)] + part_in[j, :, pl.ds(0, ff)]) * scale[0:1]
            up = (part_out[j, :, pl.ds(ff, ff)] + part_in[j, :, pl.ds(ff, ff)]) * scale[1:2]
            units = (gate / (1.0 + jnp.exp(-gate)) * up).astype(jnp.bfloat16)
            down_copy(j, slot).wait()
            values[pl.ds(pl.multiple_of(j * slots, slots), slots), :] = jnp.dot(
                units, down_buf[slot], preferred_element_type=jnp.float32
            ).astype(jnp.bfloat16)

            @pl.when(j + down_ring < held)
            def _():
                down_copy(j + down_ring, slot).start()

    rows_f32[...] = jnp.dot(mixing, values[...], preferred_element_type=jnp.float32)

    @pl.loop(0, n_ep)
    def _(b):
        both = rows_f32[pl.ds(pl.multiple_of(b * block, block), block), :]
        for h in range(n_tp):
            back_out[b * n_tp + h] = both[h * rows : (h + 1) * rows].astype(jnp.bfloat16)

    back_in[me] = back_out[me]

    @pl.loop(1, peers)
    def _(offset):
        where, peer = peer_of(offset)
        pltpu.make_async_remote_copy(
            src_ref=back_out.at[peer],
            dst_ref=back_in.at[me],
            send_sem=plain_sem.at[4],
            recv_sem=plain_sem.at[5],
            device_id=where,
            device_id_type=MESH,
        ).start()

    @pl.loop(0, held)
    def _(j):
        part_copy(j).wait_send()

    drain(route_in, n_ep - 1, plain_sem.at[0])
    drain(row_in, peers - 1, plain_sem.at[2])
    drain(back_in, peers - 1, plain_sem.at[5])
    for h in range(n_tp):
        def add(e, total):
            return total + back_in[e * n_tp + h].astype(jnp.float32)

        total = lax.fori_loop(0, n_ep, add, jnp.zeros((rows, half), jnp.float32))
        out_ref[:, h * half : (h + 1) * half] = total.astype(jnp.bfloat16)
    drain(back_in, peers - 1, plain_sem.at[4])


def body(
    hidden,
    norm_gain,
    rot_left,
    rot_right,
    expert_ids,
    gate_weights,
    w_gate,
    w_up,
    w_down,
    unit_scales,
):
    n_ep, n_tp = lax.axis_size("ep"), lax.axis_size("tp")
    peers = n_ep * n_tp
    rows, width = hidden.shape
    group_rows, choices = expert_ids.shape
    held, half, ff = w_gate.shape
    experts = held * n_ep // 2
    capacity = 5 * group_rows * choices // (2 * experts)
    slots = capacity * n_ep
    total_rows = n_ep * group_rows
    unit_ring, down_ring = min(UNIT_RING, held), min(DOWN_RING, held)
    vmem = pl.BlockSpec(memory_space=pltpu.VMEM)
    hbm = pl.BlockSpec(memory_space=pl.ANY)
    return pl.pallas_call(
        functools.partial(kernel, (n_ep, n_tp, capacity)),
        out_shape=jax.ShapeDtypeStruct((rows, width), jnp.bfloat16),
        in_specs=[vmem] * 7 + [hbm] * 3,
        out_specs=vmem,
        scratch_shapes=[
            pltpu.VMEM((unit_ring, half, ff), jnp.bfloat16),
            pltpu.VMEM((unit_ring, half, ff), jnp.bfloat16),
            pltpu.VMEM((down_ring, ff, half), jnp.bfloat16),
            pltpu.VMEM((n_tp, rows, half), jnp.bfloat16),
            pltpu.VMEM((peers, rows, half), jnp.bfloat16),
            pltpu.VMEM((group_rows, capacity * experts), jnp.float32),
            pltpu.VMEM((n_ep, group_rows, capacity * experts), jnp.float32),
            pltpu.VMEM((total_rows, half), jnp.float32),
            pltpu.VMEM((capacity * experts, total_rows), jnp.float32),
            pltpu.VMEM((held, slots, half), jnp.bfloat16),
            pltpu.VMEM((held, slots, 2 * ff), jnp.float32),
            pltpu.VMEM((held, slots, 2 * ff), jnp.float32),
            pltpu.VMEM((held * slots, half), jnp.bfloat16),
            pltpu.VMEM((peers, rows, half), jnp.bfloat16),
            pltpu.VMEM((peers, rows, half), jnp.bfloat16),
            pltpu.SemaphoreType.DMA((unit_ring,)),
            pltpu.SemaphoreType.DMA((unit_ring,)),
            pltpu.SemaphoreType.DMA((down_ring,)),
            pltpu.SemaphoreType.DMA((held,)),
            pltpu.SemaphoreType.DMA((held,)),
            pltpu.SemaphoreType.DMA((6,)),
        ],
        compiler_params=pltpu.CompilerParams(
            collective_id=0, has_side_effects=True, vmem_limit_bytes=62 * 1024 * 1024
        ),
    )(
        hidden,
        norm_gain.reshape(1, width),
        rot_left,
        rot_right,
        expert_ids,
        gate_weights,
        unit_scales,
        w_gate,
        w_up,
        w_down,
    )


def solution(mesh):
    placed = (
        P(("groups", "ep", "tp"), None),
        P(),
        P(),
        P(),
        P(("groups", "ep"), None),
        P(("groups", "ep"), None),
        P("ep", "tp", None),
        P("ep", "tp", None),
        P("ep", None, "tp"),
        P("ep", None, None),
    )
    return jax.shard_map(
        body, mesh=mesh, in_specs=placed, out_specs=P(("groups", "ep", "tp"), None), check_vma=False
    )
```

time: 140 us -> 38.1 us (0.27)
  blocking collectives: 39.1 us -> 0 us
  Pallas kernels: 0 us -> 36.5 us
  matrix products: 33.7 us -> 0 us
  waiting for transfers between devices: 33.1 us -> 0 us
  between operations: 13.6 us -> 0.01 us
  starting transfers between devices: 9.08 us -> 0 us
  local copies, waits for them, and re-layouts: 6.33 us -> 1.39 us
  other arithmetic: 4.44 us -> 0 us
    all_to_all x2 -> x0, blocking collectives: 37.2 us -> none  [the longest x1 33.4 us: body(): lax.all_to_all(outgoing, 'ep', split_axis=0, concat_axis=0, tiled=True)]
    pallas_call x0 -> x1, Pallas kernels: none -> 36.5 us  [body(): pl.pallas_call(functools.partial(kernel, (n_ep, n_tp, capacity)), out_sha...]
    dot_general x7 -> x0, matrix products: 33.7 us -> none  [the longest x1 11.5 us: body(): jnp.einsum('shcf,hfd->shcd', hidden_units, w_down, preferred_element_type...]
    all_to_all x2 -> x0, waiting for transfers between devices: 26 us -> none  [the longest x1 26 us: body(): lax.all_to_all(flat_partial, 'ep', split_axis=0, concat_axis=0, tiled=True)]
    all_to_all x2 -> x0, starting transfers between devices: 8.99 us -> none  [the longest x1 5.74 us: body(): lax.all_to_all(flat_partial, 'ep', split_axis=0, concat_axis=0, tiled=True)]
    reduce_scatter x2 -> x0, waiting for transfers between devices: 7.1 us -> none  [the longest x1 7.08 us: body(): lax.psum_scatter(up_sum, 'tp', scatter_dimension=0, tiled=True)]
    all_gather x1 -> x0, blocking collectives: 1.95 us -> none  [body(): hidden_units = lax.all_gather(half_hidden, 'tp', axis=0, tiled=True)]
    reshape x3 -> x0, local copies, waits for them, and re-layouts: 1.78 us -> none  [the longest x1 1.58 us: body(): flat_partial = partial_value.reshape(ep_count, held_halves * capacity, -1)]
  transfers between devices with their start and end apart: 4 -> 0, of which waited for: 2 -> 0; matrix products, arithmetic and copies ran while one was open for 9% -> 0% of each run, Pallas kernels for 0% -> 0%
where the time goes in v1:
time: 38.1 us; the launch traced here: 37.9 us
  Pallas kernels  36.5 us (96%)
  local copies, waits for them, and re-layouts  1.39 us (4%)
    pallas_call x1, Pallas kernels, body(): pl.pallas_call(functools.partial(kernel, (n_ep, n_tp, capacity)), out_sha...  36.5 us
    unnamed x1, local copies, waits for them, and re-layouts  1.39 us

profile of v1, /device:TPU:0, one launch (start us, length us, event | category | flops | bytes accessed | tf_op | source)
XLA Modules:
  0.0 37.9 jit_solution(13674756736429877058)
XLA Ops:
  0.0 36.5 %shard_map.100 = bf16[4,4096]{1,0:T(4,128)(2,1)} custom-call(bf16[4,4096]{1,0:T(4,128)(2,1)} %hid_ref.1, f32[1,4096]{1,0:T(1,128)} %bitcast.1, f32[64,64]{1,0:T(8,128)} %left_ref.1, f32[64,64]{1,0:T(8,128)} %right_ref.1, s32[8,8]{1,0:T(8,128)} %ids_ref.1, f32[8,8]{1,0:T(8,128)} %weights_ref.1, f32[16,2,384]{2,1,0:T(2,128)} %scales_ref.1, ...), custom_call_target="tpu_custom_call" | custom-call | tf_op jit(solution)/shard_map/pallas_call | solution.py:340
  36.5 1.4 %copy.12 = bf16[4,4096]{1,0:T(4,128)(2,1)} copy(bf16[4,4096]{1,0:T(4,128)(2,1)} %shard_map.100) | data formatting | bytes 65536

commit v2 on v1

--- a/solution.py
+++ b/solution.py
@@ -12,7 +12,7 @@
 LANES = 128
 LAG = 3
 UNIT_RING = 10
-DOWN_RING = 8
+CHUNK = 512
 
 
 def iota(shape, dim):
@@ -111,7 +111,9 @@
     lines,
     part_out,
     part_in,
+    units,
     values,
+    mixed,
     back_out,
     back_in,
     gate_sem,
@@ -120,6 +122,8 @@
     part_send,
     part_recv,
     plain_sem,
+    back_send,
+    back_recv,
 ):
     n_ep, n_tp, capacity = sizes
     peers = n_ep * n_tp
@@ -128,7 +132,7 @@
     me = ep * n_tp + tp
     held = gate_hbm.shape[0]
     unit_ring = gate_buf.shape[0]
-    down_ring = down_buf.shape[0]
+    chunks, chunk = down_buf.shape[0], down_buf.shape[3]
     rows = hid_ref.shape[0]
     half = row_in.shape[2]
     block = rows * n_tp
@@ -143,15 +147,16 @@
             pltpu.make_async_copy(up_hbm.at[j], up_buf.at[slot], up_sem.at[slot]),
         )
 
-    def down_copy(j, slot):
-        return pltpu.make_async_copy(down_hbm.at[j], down_buf.at[slot], down_sem.at[slot])
-
-    for j in range(max(unit_ring, down_ring + LAG)):
-        if j < unit_ring:
-            for copy in unit_copies(j, j):
-                copy.start()
-        if LAG <= j < down_ring + LAG:
-            down_copy(j - LAG, j - LAG).start()
+    def down_copy(c):
+        return pltpu.make_async_copy(
+            down_hbm.at[:, :, pl.ds(c * chunk, chunk)], down_buf.at[c], down_sem.at[c]
+        )
+
+    for j in range(unit_ring):
+        for copy in unit_copies(j, j):
+            copy.start()
+    for c in range(chunks):
+        down_copy(c).start()
 
     barrier = pltpu.get_barrier_semaphore()
 
@@ -236,66 +241,83 @@
             device_id_type=MESH,
         )
 
-    @pl.loop(0, held + LAG)
+    def project(t, slot):
+        line = lines[t]
+        gate = jnp.dot(line, gate_buf[slot], preferred_element_type=jnp.float32)
+        up = jnp.dot(line, up_buf[slot], preferred_element_type=jnp.float32)
+        return gate, up
+
+    def send(t, gate, up):
+        part_out[t, :, pl.ds(0, ff)] = gate
+        part_out[t, :, pl.ds(ff, ff)] = up
+        part_copy(t).start()
+
+    def activate(j):
+        scale = scales_ref[j]
+        gate = (part_out[j, :, pl.ds(0, ff)] + part_in[j, :, pl.ds(0, ff)]) * scale[0:1]
+        up = (part_out[j, :, pl.ds(ff, ff)] + part_in[j, :, pl.ds(ff, ff)]) * scale[1:2]
+        units[j] = (gate / (1.0 + jnp.exp(-gate)) * up).astype(jnp.bfloat16)
+
+    def refill(t, slot):
+        @pl.when(t + unit_ring < held)
+        def _():
+            for copy in unit_copies(t + unit_ring, slot):
+                copy.start()
+
+    lag = min(LAG, held)
+
+    @pl.loop(0, lag)
     def _(t):
-        @pl.when(t < held)
-        def _():
-            slot = lax.rem(t, unit_ring)
-            for copy in unit_copies(t, slot):
-                copy.wait()
-            line = lines[t]
-            part_out[t, :, pl.ds(0, ff)] = jnp.dot(
-                line, gate_buf[slot], preferred_element_type=jnp.float32
-            )
-            part_out[t, :, pl.ds(ff, ff)] = jnp.dot(
-                line, up_buf[slot], preferred_element_type=jnp.float32
-            )
-            part_copy(t).start()
-
-            @pl.when(t + unit_ring < held)
-            def _():
-                for copy in unit_copies(t + unit_ring, slot):
-                    copy.start()
-
-        @pl.when(t >= LAG)
-        def _():
-            j = t - LAG
-            slot = lax.rem(j, down_ring)
-            part_copy(j).wait_recv()
-            scale = scales_ref[j]
-            gate = (part_out[j, :, pl.ds(0, ff)] + part_in[j, :, pl.ds(0, ff)]) * scale[0:1]
-            up = (part_out[j, :, pl.ds(ff, ff)] + part_in[j, :, pl.ds(ff, ff)]) * scale[1:2]
-            units = (gate / (1.0 + jnp.exp(-gate)) * up).astype(jnp.bfloat16)
-            down_copy(j, slot).wait()
-            values[pl.ds(pl.multiple_of(j * slots, slots), slots), :] = jnp.dot(
-                units, down_buf[slot], preferred_element_type=jnp.float32
-            ).astype(jnp.bfloat16)
-
-            @pl.when(j + down_ring < held)
-            def _():
-                down_copy(j + down_ring, slot).start()
-
-    rows_f32[...] = jnp.dot(mixing, values[...], preferred_element_type=jnp.float32)
-
-    @pl.loop(0, n_ep)
-    def _(b):
-        both = rows_f32[pl.ds(pl.multiple_of(b * block, block), block), :]
-        for h in range(n_tp):
-            back_out[b * n_tp + h] = both[h * rows : (h + 1) * rows].astype(jnp.bfloat16)
-
-    back_in[me] = back_out[me]
-
-    @pl.loop(1, peers)
-    def _(offset):
+        for copy in unit_copies(t, t):
+            copy.wait()
+        send(t, *project(t, t))
+        refill(t, t)
+
+    @pl.loop(lag, held)
+    def _(t):
+        slot = lax.rem(t, unit_ring)
+        for copy in unit_copies(t, slot):
+            copy.wait()
+        part_copy(t - lag).wait_recv()
+        activate(t - lag)
+        send(t, *project(t, slot))
+        refill(t, slot)
+
+    for j in range(held - lag, held):
+        part_copy(j).wait_recv()
+        activate(j)
+
+    def back_copy(c, offset):
         where, peer = peer_of(offset)
-        pltpu.make_async_remote_copy(
-            src_ref=back_out.at[peer],
-            dst_ref=back_in.at[me],
-            send_sem=plain_sem.at[4],
-            recv_sem=plain_sem.at[5],
+        return pltpu.make_async_remote_copy(
+            src_ref=back_out.at[c, peer],
+            dst_ref=back_in.at[c, me],
+            send_sem=back_send.at[c],
+            recv_sem=back_recv.at[c],
             device_id=where,
             device_id_type=MESH,
-        ).start()
+        )
+
+    @pl.loop(0, chunks)
+    def _(c):
+        down_copy(c).wait()
+        for j in range(held):
+            values[j * slots : (j + 1) * slots] = jnp.dot(
+                units[j], down_buf[c, j], preferred_element_type=jnp.float32
+            ).astype(jnp.bfloat16)
+        mixed[...] = jnp.dot(mixing, values[...], preferred_element_type=jnp.float32)
+
+        @pl.loop(0, n_ep)
+        def _(b):
+            both = mixed[pl.ds(pl.multiple_of(b * block, block), block), :]
+            for h in range(n_tp):
+                back_out[c, b * n_tp + h] = both[h * rows : (h + 1) * rows].astype(jnp.bfloat16)
+
+        @pl.loop(1, peers)
+        def _(offset):
+            back_copy(c, offset).start()
+
+        back_in[c, me] = back_out[c, me]
 
     @pl.loop(0, held)
     def _(j):
@@ -303,14 +325,18 @@
 
     drain(route_in, n_ep - 1, plain_sem.at[0])
     drain(row_in, peers - 1, plain_sem.at[2])
-    drain(back_in, peers - 1, plain_sem.at[5])
-    for h in range(n_tp):
-        def add(e, total):
-            return total + back_in[e * n_tp + h].astype(jnp.float32)
-
-        total = lax.fori_loop(0, n_ep, add, jnp.zeros((rows, half), jnp.float32))
-        out_ref[:, h * half : (h + 1) * half] = total.astype(jnp.bfloat16)
-    drain(back_in, peers - 1, plain_sem.at[4])
+    for c in range(chunks):
+        drain(back_in.at[c], peers - 1, back_recv.at[c])
+        for h in range(n_tp):
+
+            def add(e, total):
+                return total + back_in[c, e * n_tp + h].astype(jnp.float32)
+
+            total = lax.fori_loop(0, n_ep, add, jnp.zeros((rows, chunk), jnp.float32))
+            start = h * half + c * chunk
+            out_ref[:, start : start + chunk] = total.astype(jnp.bfloat16)
+    for c in range(chunks):
+        drain(back_in.at[c], peers - 1, back_send.at[c])
 
 
 def body(
@@ -334,7 +360,9 @@
     capacity = 5 * group_rows * choices // (2 * experts)
     slots = capacity * n_ep
     total_rows = n_ep * group_rows
-    unit_ring, down_ring = min(UNIT_RING, held), min(DOWN_RING, held)
+    unit_ring = min(UNIT_RING, held)
+    chunk = min(CHUNK, half)
+    chunks = half // chunk
     vmem = pl.BlockSpec(memory_space=pltpu.VMEM)
     hbm = pl.BlockSpec(memory_space=pl.ANY)
     return pl.pallas_call(
@@ -345,7 +373,7 @@
         scratch_shapes=[
             pltpu.VMEM((unit_ring, half, ff), jnp.bfloat16),
             pltpu.VMEM((unit_ring, half, ff), jnp.bfloat16),
-            pltpu.VMEM((down_ring, ff, half), jnp.bfloat16),
+            pltpu.VMEM((chunks, held, ff, chunk), jnp.bfloat16),
             pltpu.VMEM((n_tp, rows, half), jnp.bfloat16),
             pltpu.VMEM((peers, rows, half), jnp.bfloat16),
             pltpu.VMEM((group_rows, capacity * experts), jnp.float32),
@@ -355,18 +383,22 @@
             pltpu.VMEM((held, slots, half), jnp.bfloat16),
             pltpu.VMEM((held, slots, 2 * ff), jnp.float32),
             pltpu.VMEM((held, slots, 2 * ff), jnp.float32),
-            pltpu.VMEM((held * slots, half), jnp.bfloat16),
-            pltpu.VMEM((peers, rows, half), jnp.bfloat16),
-            pltpu.VMEM((peers, rows, half), jnp.bfloat16),
+            pltpu.VMEM((held, slots, ff), jnp.bfloat16),
+            pltpu.VMEM((held * slots, chunk), jnp.bfloat16),
+            pltpu.VMEM((total_rows, chunk), jnp.float32),
+            pltpu.VMEM((chunks, peers, rows, chunk), jnp.bfloat16),
+            pltpu.VMEM((chunks, peers, rows, chunk), jnp.bfloat16),
             pltpu.SemaphoreType.DMA((unit_ring,)),
             pltpu.SemaphoreType.DMA((unit_ring,)),
-            pltpu.SemaphoreType.DMA((down_ring,)),
+            pltpu.SemaphoreType.DMA((chunks,)),
             pltpu.SemaphoreType.DMA((held,)),
             pltpu.SemaphoreType.DMA((held,)),
-            pltpu.SemaphoreType.DMA((6,)),
+            pltpu.SemaphoreType.DMA((4,)),
+            pltpu.SemaphoreType.DMA((chunks,)),
+            pltpu.SemaphoreType.DMA((chunks,)),
         ],
         compiler_params=pltpu.CompilerParams(
-            collective_id=0, has_side_effects=True, vmem_limit_bytes=62 * 1024 * 1024
+            collective_id=0, has_side_effects=True, vmem_limit_bytes=63 * 1024 * 1024
         ),
     )(
         hidden,

time: 38.1 us -> 40.9 us (1.073)
  Pallas kernels: 36.5 us -> 39.3 us
    pallas_call x1, Pallas kernels: 36.5 us -> 39.3 us  [body(): pl.pallas_call(functools.partial(kernel, (n_ep, n_tp, capacity)), out_sha...]
where the time goes in v2:
time: 40.9 us; the launch traced here: 40.7 us
  Pallas kernels  39.3 us (96%)
  local copies, waits for them, and re-layouts  1.39 us (3%)
    pallas_call x1, Pallas kernels, body(): pl.pallas_call(functools.partial(kernel, (n_ep, n_tp, capacity)), out_sha...  39.3 us
    unnamed x1, local copies, waits for them, and re-layouts  1.39 us

profile of v2, /device:TPU:0, one launch (start us, length us, event | category | flops | bytes accessed | tf_op | source)
XLA Modules:
  0.0 40.7 jit_solution(14053101364899908411)
XLA Ops:
  0.0 39.3 %shard_map.100 = bf16[4,4096]{1,0:T(4,128)(2,1)} custom-call(bf16[4,4096]{1,0:T(4,128)(2,1)} %hid_ref.1, f32[1,4096]{1,0:T(1,128)} %bitcast.1, f32[64,64]{1,0:T(8,128)} %left_ref.1, f32[64,64]{1,0:T(8,128)} %right_ref.1, s32[8,8]{1,0:T(8,128)} %ids_ref.1, f32[8,8]{1,0:T(8,128)} %weights_ref.1, f32[16,2,384]{2,1,0:T(2,128)} %scales_ref.1, ...), custom_call_target="tpu_custom_call" | custom-call | tf_op jit(solution)/shard_map/pallas_call | solution.py:368
  39.3 1.4 %copy.12 = bf16[4,4096]{1,0:T(4,128)(2,1)} copy(bf16[4,4096]{1,0:T(4,128)(2,1)} %shard_map.100) | data formatting | bytes 65536
